TPU v7x, 32 devices: a whole 2x2x4 slice. The times are simulated.
32 devices in a mesh: row: 4 (over x, core), col: 8 (over z, y).
Axes of the slice: x: 2, y: 2, z: 4, core: 2. Of those that a mesh axis runs over, the one named last changes fastest.
Arguments:
- trailing: float32 [4096, 4096], P('row', 'col'), may hold values from -6 to 6
- panel_left: float32 [4096, 384], P(('row', 'col')), may hold values from -0.3125 to 0.3125
- panel_right: float32 [8, 1024, 384], P('row', 'col'), may hold values from -1 to 1
- panel_solved: float32 [1024, 1024], P('row', 'col'), may hold values from -1.75 to 1.75
- right_sides: float32 [4096, 1024], P('row', 'col'), may hold values from -6 to 6
- tile_ranks: int32 [8], replicated, may hold values from 64 to 384, as said below
- tile_order: int32 [8], replicated, may hold values from 0 to 7, each once
Outputs:
- trail_new: float32 [4096, 4096], P('row', 'col')
- rhs_new: float32 [4096, 1024], P('row', 'col')
Inputs may be any that keep to these rules, and one draw needn't show every extreme that they name: `tile_ranks`: every rank is a multiple of 64; both 64 and 384 occur in every draw. `tile_order`: each tile appears in exactly one slot.
All inputs are finite; a program needn't handle non-finite values.
Results may differ from a plain program's by a relative error of at most 0.00008.
Values sent between devices are 32-bit elements; how exact they have to be, the bound alone decides.
A program may use at most 64 MiB of HBM per device.

v0:
```python
import jax
import jax.numpy as jnp
from jax import lax
from jax.sharding import PartitionSpec as P


def spread(value, axis, root):
    mine = lax.axis_index(axis) == root
    return lax.psum(jnp.where(mine, value, jnp.zeros_like(value)), axis)


def exact_dot(left, right):
    return jnp.dot(left, right, precision=lax.Precision.HIGHEST, preferred_element_type=jnp.float32)


def on_device(trailing, panel_left, panel_right, panel_solved, right_sides, tile_ranks, tile_order):
    slot_count = panel_right.shape[0]
    tile_count = tile_order.shape[0]
    rank_width = panel_left.shape[1]
    left_rows, right_rows = (
        lax.all_gather(panel_left, "col", axis=0, tiled=True),
        lax.all_gather(panel_right, "col", axis=1, tiled=True),
    )
    tile_rows = left_rows.shape[0] // slot_count
    left_rows = left_rows.reshape(slot_count, tile_rows, rank_width)
    row_index = lax.axis_index("row")
    column = lax.axis_index("col")
    places = jnp.arange(tile_count, dtype=jnp.int32)
    levels = jnp.arange(rank_width, dtype=jnp.int32)
    slot_ids = row_index * slot_count + jnp.arange(slot_count, dtype=jnp.int32)
    my_tiles = jnp.sum(
        jnp.where(places[None, :] == slot_ids[:, None], tile_order[None, :], 0), axis=1
    )
    my_ranks = jnp.sum(
        jnp.where(places[None, :] == my_tiles[:, None], tile_ranks[None, :], 0), axis=1
    )
    keep_mask = (levels[None, :] < my_ranks[:, None]).astype(jnp.float32)
    left_mine = left_rows * keep_mask[:, None, :]
    root_slot = jnp.sum(jnp.where(tile_order == column, places, 0))
    root_row = root_slot // slot_count
    local_slot = root_slot % slot_count
    column_rank = jnp.sum(jnp.where(places == column, tile_ranks, 0))
    column_mask = (levels < column_rank).astype(jnp.float32)
    left_pick = (
        lax.dynamic_index_in_dim(left_rows, local_slot, 0, keepdims=False) * column_mask[None, :]
    )
    right_pick = lax.dynamic_index_in_dim(right_rows, local_slot, 0, keepdims=False)

    def owner_panel():
        return exact_dot(right_pick, left_pick.T)

    def other_panel():
        return jnp.zeros((right_pick.shape[0], tile_rows), jnp.float32)

    column_dense = lax.cond(row_index == root_row, owner_panel, other_panel)
    column_dense = spread(column_dense, "row", root_row)
    solved = jnp.einsum(
        "snk,nj->skj",
        right_rows,
        lax.all_gather(panel_solved, "row", axis=0, tiled=True),
        precision=lax.Precision.HIGHEST,
        preferred_element_type=jnp.float32,
    )
    updates = []
    for slot in range(slot_count):
        left_part = left_mine[slot]
        slot_right_part = right_rows[slot]
        middle = exact_dot(slot_right_part.T, column_dense)
        updates.append(exact_dot(left_part, jnp.concatenate([middle, solved[slot]], 1)))
    update_all = jnp.concatenate(updates, 0)
    trail_new = trailing - update_all[:, :tile_rows]
    rhs_new = right_sides - update_all[:, tile_rows:]
    return (trail_new, rhs_new)


def solution(mesh):
    return jax.shard_map(
        on_device,
        mesh=mesh,
        in_specs=(
            P("row", "col"),
            P(("row", "col"), None),
            P("row", "col", None),
            P("row", "col"),
            P("row", "col"),
            P(),
            P(),
        ),
        out_specs=(P("row", "col"), P("row", "col")),
        check_vma=False,
    )
```

profile of v0, /device:TPU:0, one launch (start us, length us, event | category | flops | bytes accessed | tf_op | source)
XLA Modules:
  0.0 198.6 jit_solution(3108771299947774375)
XLA Ops:
  7.2 0.7 all-gather.3.cloned.1.call-update
  7.9 0.7 all-gather.5.cloned.1.call-update
  8.7 1.3 fusion.27
  12.6 1.0 copy.10
  13.6 1.3 fusion.28
  14.9 0.6 compare_convert_fusion
  15.6 0.8 fusion.25
  16.4 0.8 fusion.26
  17.3 39.8 %all-gather.3.cloned.1.call-done = f32[1024,384]{1,0:T(8,128)} async-done(((f32[128,384]{1,0:T(8,128)}), f32[1024,384]{1,0:T(8,128)}) %all-gather.3.cloned.1.call-update) | async-done | bytes 1572880 | tf_op jit(solution)/shard_map/all_gather | solution.py:21
  57.1 60.6 %all-gather.5.cloned.1.call-done = f32[2,1024,384]{2,1,0:T(8,128)} async-done(((f32[2,128,384]{2,1,0:T(8,128)}), f32[2,1024,384]{2,1,0:T(8,128)}) %all-gather.5.cloned.1.call-update) | async-done | bytes 3145744 | tf_op jit(solution)/shard_map/all_gather | solution.py:22
  117.7 0.3 conditional.1
  117.7 0.2 broadcast.35
  118.0 1.5 broadcast_select_fusion
  119.5 12.9 %all_gather.11 = f32[1024,128]{0,1:T(8,128)S(1)} all-gather(f32[256,128]{0,1:T(8,128)S(1)} %copy.10), channel_id=1, replica_groups=mesh['row'=4,'col'=8] {'row'}, dimensions={0}, use_global_device_ids=true | all-gather | bytes 655360 | tf_op jit(solution)/shard_map/all_gather | solution.py:60
  132.4 2.7 %broadcast_multiply_fusion = f32[2,512,384]{2,1,0:T(8,128)} fusion(f32[2,512,384]{2,1,0:T(8,128)} %bitcast.38, f32[2,384]{1,0:T(2,128)S(1)} %compare_convert_fusion.1), kind=kLoop, calls=%fused_computation.29 | loop fusion | flops 393216 | bytes 3148800 | tf_op jit(solution)/shard_map/mul | solution.py:38
  135.1 1.9 fusion.23
  137.1 37.5 %all-reduce.2.cloned.1.call-done = f32[1024,512]{1,0:T(8,128)} async-done(((f32[1024,512]{1,0:T(8,128)}), f32[1024,512]{1,0:T(8,128)}) %all-reduce.2.cloned.1.call-update) | async-done | bytes 2097168 | tf_op jit(solution)/shard_map/psum | solution.py:9
  174.5 5.2 %fusion.13 = f32[384,512]{0,1:T(8,128)S(1)} fusion(f32[1024,512]{1,0:T(8,128)} %all-reduce.2.cloned.1.call-done, f32[2,1024,384]{2,1,0:T(8,128)S(1)} %copy-done), kind=kOutput, calls=%fused_computation.17 | convolution fusion | flops 2415919104 | bytes 4456448 | tf_op jit(solution)/shard_map/dot_general | solution.py:13
  179.7 2.5 %fusion.18 = f32[512,640]{1,0:T(8,128)S(1)} fusion(f32[384,128]{0,1:T(8,128)S(1)} %get-tuple-element.85, f32[384,512]{0,1:T(8,128)S(1)} %fusion.13, f32[2,512,384]{2,1,0:T(8,128)S(1)} %copy-done.2), kind=kOutput, calls=%fused_computation.23 | convolution fusion | flops 1510195200 | bytes 3080192 | tf_op jit(solution)/shard_map/dot_general | solution.py:13
  182.3 3.8 %fusion.12 = f32[384,512]{0,1:T(8,128)S(1)} fusion(f32[1024,512]{1,0:T(8,128)S(1)} %copy-done.1, f32[2,1024,384]{2,1,0:T(8,128)S(1)} %copy-done), kind=kOutput, calls=%fused_computation.16 | convolution fusion | flops 2415919104 | bytes 4456448 | tf_op jit(solution)/shard_map/dot_general | solution.py:13
  186.1 2.5 %fusion.14 = f32[512,640]{1,0:T(8,128)S(1)} fusion(f32[384,128]{0,1:T(8,128)S(1)} %get-tuple-element.86, f32[384,512]{0,1:T(8,128)S(1)} %fusion.12, f32[2,512,384]{2,1,0:T(8,128)S(1)} %copy-done.2), kind=kOutput, calls=%fused_computation.19 | convolution fusion | flops 1510195200 | bytes 3080192 | tf_op jit(solution)/shard_map/dot_general | solution.py:13
  188.6 0.9 fusion.22
  189.5 0.9 copy-done.3
  190.4 1.6 fusion.9
  (16 shorter events, 0.3 us)
Async XLA Ops:
  7.2 49.9 %all-gather.3.cloned.1.call-start = ((), (), s32[]{:S(2)}) async-start(), calls=%async_computation | async-start | bytes 1769472 | tf_op jit(solution)/shard_map/all_gather | solution.py:21
  7.9 109.8 %all-gather.5.cloned.1.call-start = ((), (), s32[]{:S(2)}) async-start(), calls=%async_computation.1 | async-start | bytes 3538944 | tf_op jit(solution)/shard_map/all_gather | solution.py:22
  8.6 165.9 %all-reduce.2.cloned.1.call-start = ((), (), s32[]{:S(2)}) async-start(), calls=%async_computation.2 | async-start | bytes 4194304 | tf_op jit(solution)/shard_map/psum | solution.py:9
  119.5 15.6 %copy-start = (f32[2,1024,384]{2,1,0:T(8,128)S(1)}, f32[2,1024,384]{2,1,0:T(8,128)}, u32[]{:S(2)}) copy-start(f32[2,1024,384]{2,1,0:T(8,128)} %all-gather.5.cloned.1.call-done) | copy-start | bytes 9437188
  174.5 5.2 %copy-start.2 = (f32[2,512,384]{2,1,0:T(8,128)S(1)}, f32[2,512,384]{2,1,0:T(8,128)}, u32[]{:S(2)}) copy-start(f32[2,512,384]{2,1,0:T(8,128)} %broadcast_multiply_fusion) | copy-start | bytes 4718596
  179.7 2.5 %copy-start.1 = (f32[1024,512]{1,0:T(8,128)S(1)}, f32[1024,512]{1,0:T(8,128)}, u32[]{:S(2)}) copy-start(f32[1024,512]{1,0:T(8,128)} %all-reduce.2.cloned.1.call-done) | copy-start | bytes 6291460
  186.1 2.5 %copy-start.4 = (f32[1024,128]{1,0:T(8,128)S(1)}, f32[1024,128]{1,0:T(8,128)}, u32[]{:S(2)}) copy-start(f32[1024,128]{1,0:T(8,128)} %param.13) | copy-start | bytes 1572868
  188.6 1.8 copy-start.3
Sparse Core Ops, SparseCore 0:
  10.2 46.8 all-gather.2
  59.3 58.3 all-gather.4
  120.6 53.8 all-reduce.1
where the time goes:
time: 199 us
  waiting for transfers between devices  139 us (70%)
  between operations  16.5 us (8%)
  matrix products  15.9 us (8%)
  blocking collectives  12.9 us (6%)
  other arithmetic  11.7 us (6%)
  local copies, waits for them, and re-layouts  2.21 us (1%)
    all_gather x1, waiting for transfers between devices, on_device(): lax.all_gather(panel_right, 'col', axis=1, tiled=True)  60.6 us
    all_gather x1, waiting for transfers between devices, on_device(): lax.all_gather(panel_left, 'col', axis=0, tiled=True)  39.8 us
    psum x1, waiting for transfers between devices, spread(): return lax.psum(jnp.where(mine, value, jnp.zeros_like(value)), axis)  37.5 us
    dot_general x4, matrix products, exact_dot(): jnp.dot(left, right, precision=lax.Precision.HIGHEST, preferred_element_t...  14 us
    all_gather x1, blocking collectives, on_device(): lax.all_gather(panel_solved, 'row', axis=0, tiled=True)  12.9 us
  transfers between devices with their start and end apart: 3, of which 3 were waited for; matrix products, arithmetic and copies ran while one was open for 5% of the time, Pallas kernels for 0%

commit v1 on v0

--- a/solution.py
+++ b/solution.py
@@ -2,6 +2,22 @@
 import jax.numpy as jnp
 from jax import lax
 from jax.sharding import PartitionSpec as P
+
+
+def product_in_turn(shard, axis, dim, product):
+    size, index, rows = (lax.axis_size(axis), lax.axis_index(axis), shard.shape[dim])
+    forward = [(i, (i + 1) % size) for i in range(size)]
+    behind = [(i, (i - 1) % size) for i in range(size)]
+    half = size // 2
+    from_left = from_right = shard
+    running = product(shard, index * rows)
+    for turn in range(1, half + 1):
+        from_left = lax.ppermute(from_left, axis, forward)
+        if turn < size - half:
+            from_right = lax.ppermute(from_right, axis, behind)
+            running = running + product(from_right, (index + turn) % size * rows)
+        running = running + product(from_left, (index - turn) % size * rows)
+    return running
 
 
 def spread(value, axis, root):
@@ -54,12 +70,17 @@
 
     column_dense = lax.cond(row_index == root_row, owner_panel, other_panel)
     column_dense = spread(column_dense, "row", root_row)
-    solved = jnp.einsum(
-        "snk,nj->skj",
-        right_rows,
-        lax.all_gather(panel_solved, "row", axis=0, tiled=True),
-        precision=lax.Precision.HIGHEST,
-        preferred_element_type=jnp.float32,
+    solved = product_in_turn(
+        panel_solved,
+        "row",
+        0,
+        lambda part, offset: jnp.einsum(
+            "snk,nj->skj",
+            lax.dynamic_slice_in_dim(right_rows, offset, part.shape[0], axis=1),
+            part,
+            precision=lax.Precision.HIGHEST,
+            preferred_element_type=jnp.float32,
+        ),
     )
     updates = []
     for slot in range(slot_count):

time: 199 us -> 202 us (1.015)
  blocking collectives: 12.9 us -> 0 us
  waiting for transfers between devices: 139 us -> 147 us
  local copies, waits for them, and re-layouts: 2.21 us -> 5.39 us
  starting transfers between devices: 0.11 us -> 3.25 us
    psum x1, waiting for transfers between devices: 37.5 us -> 52.2 us  [spread(): return lax.psum(jnp.where(mine, value, jnp.zeros_like(value)), axis)]
    all_gather x1 -> x0, blocking collectives: 12.9 us -> none  [on_device(): lax.all_gather(panel_solved, 'row', axis=0, tiled=True)]
    all_gather x1, waiting for transfers between devices: 39.8 us -> 35.9 us  [on_device(): lax.all_gather(panel_left, 'col', axis=0, tiled=True)]
    unnamed x11 -> x15, local copies, waits for them, and re-layouts: 1.93 us -> 5.11 us
    ppermute x0 -> x3, starting transfers between devices: none -> 3.14 us  [the longest x1 2.41 us: product_in_turn(): from_right = lax.ppermute(from_right, axis, behind)]
    all_gather x1, waiting for transfers between devices: 60.6 us -> 57.9 us  [on_device(): lax.all_gather(panel_right, 'col', axis=1, tiled=True)]
  transfers between devices with their start and end apart: 3 -> 6, of which waited for: 3 -> 3; matrix products, arithmetic and copies ran while one was open for 5% -> 7% of each run, Pallas kernels for 0% -> 0%
where the time goes in v1:
time: 202 us
  waiting for transfers between devices  147 us (73%)
  matrix products  17.3 us (9%)
  between operations  16.6 us (8%)
  other arithmetic  11.8 us (6%)
  local copies, waits for them, and re-layouts  5.39 us (3%)
  starting transfers between devices  3.25 us (2%)
    all_gather x1, waiting for transfers between devices, on_device(): lax.all_gather(panel_right, 'col', axis=1, tiled=True)  57.9 us
    psum x1, waiting for transfers between devices, spread(): return lax.psum(jnp.where(mine, value, jnp.zeros_like(value)), axis)  52.2 us
    all_gather x1, waiting for transfers between devices, on_device(): lax.all_gather(panel_left, 'col', axis=0, tiled=True)  35.9 us
    dot_general x4, matrix products, exact_dot(): jnp.dot(left, right, precision=lax.Precision.HIGHEST, preferred_element_t...  14 us
    unnamed x15, local copies, waits for them, and re-layouts  5.11 us
  transfers between devices with their start and end apart: 6, of which 3 were waited for; matrix products, arithmetic and copies ran while one was open for 7% of the time, Pallas kernels for 0%

profile of v1, /device:TPU:0, one launch (start us, length us, event | category | flops | bytes accessed | tf_op | source)
XLA Modules:
  0.0 201.8 jit_solution(6392189754128476521)
XLA Ops:
  7.2 0.7 all-gather.3.cloned.1.call-update
  7.9 0.7 all-gather.5.cloned.1.call-update
  8.7 1.7 copy.13
  10.4 2.4 %collective-permute-start = (f32[256,128]{0,1:T(8,128)}, f32[256,128]{0,1:T(8,128)S(1)}, u32[]{:S(2)}, u32[]{:S(2)}) collective-permute-start(f32[256,128]{0,1:T(8,128)} %copy.13), channel_id=1, source_target_pairs={{0,24},{8,0},{16,8},{24,16},{1,25},{9,1},{17,9},{25,17},{2,26},{10... | collective-permute-start | bytes 393224 | tf_op jit(solution)/shard_map/ppermute | solution.py:17
  12.8 1.3 fusion.38
  14.1 0.8 fusion.32
  14.9 0.8 fusion.33
  15.8 1.4 fusion.39
  20.5 0.7 collective-permute-start.2
  21.2 35.9 %all-gather.3.cloned.1.call-done = f32[1024,384]{1,0:T(8,128)} async-done(((f32[128,384]{1,0:T(8,128)}), f32[1024,384]{1,0:T(8,128)}) %all-gather.3.cloned.1.call-update) | async-done | bytes 1572880 | tf_op jit(solution)/shard_map/all_gather | solution.py:37
  57.1 2.7 %broadcast_multiply_fusion = f32[2,512,384]{2,1,0:T(8,128)} fusion(f32[2,512,384]{2,1,0:T(8,128)} %bitcast.45, f32[2,384]{1,0:T(2,128)S(1)} %compare_convert_fusion.1), kind=kLoop, calls=%fused_computation.37 | loop fusion | flops 393216 | bytes 3148800 | tf_op jit(solution)/shard_map/mul | solution.py:54
  59.8 57.9 %all-gather.5.cloned.1.call-done = f32[2,1024,384]{2,1,0:T(8,128)} async-done(((f32[2,128,384]{2,1,0:T(8,128)}), f32[2,1024,384]{2,1,0:T(8,128)}) %all-gather.5.cloned.1.call-update) | async-done | bytes 3145744 | tf_op jit(solution)/shard_map/all_gather | solution.py:38
  118.2 1.3 copy-done.2
  119.5 1.5 broadcast_select_fusion
  121.0 1.1 copy-done
  124.1 1.5 convolution_add_fusion
  125.6 52.2 %all-reduce.2.cloned.1.call-done = f32[1024,512]{1,0:T(8,128)} async-done(((f32[1024,512]{1,0:T(8,128)}), f32[1024,512]{1,0:T(8,128)}) %all-reduce.2.cloned.1.call-update) | async-done | bytes 2097168 | tf_op jit(solution)/shard_map/psum | solution.py:25
  177.8 5.2 %fusion.13 = f32[384,512]{0,1:T(8,128)S(1)} fusion(f32[1024,512]{1,0:T(8,128)} %all-reduce.2.cloned.1.call-done, f32[2,1024,384]{2,1,0:T(8,128)S(1)} %copy-done), kind=kOutput, calls=%fused_computation.17 | convolution fusion | flops 2415919104 | bytes 4456448 | tf_op jit(solution)/shard_map/dot_general | solution.py:29
  183.0 2.5 %fusion.18 = f32[512,640]{1,0:T(8,128)S(1)} fusion(f32[384,128]{0,1:T(8,128)S(1)} %get-tuple-element.85, f32[384,512]{0,1:T(8,128)S(1)} %fusion.13, f32[2,512,384]{2,1,0:T(8,128)S(1)} %copy-done.3), kind=kOutput, calls=%fused_computation.26 | convolution fusion | flops 1510195200 | bytes 3080192 | tf_op jit(solution)/shard_map/dot_general | solution.py:29
  185.5 3.8 %fusion.12 = f32[384,512]{0,1:T(8,128)S(1)} fusion(f32[1024,512]{1,0:T(8,128)S(1)} %copy-done.1, f32[2,1024,384]{2,1,0:T(8,128)S(1)} %copy-done), kind=kOutput, calls=%fused_computation.16 | convolution fusion | flops 2415919104 | bytes 4456448 | tf_op jit(solution)/shard_map/dot_general | solution.py:29
  189.3 2.5 %fusion.14 = f32[512,640]{1,0:T(8,128)S(1)} fusion(f32[384,128]{0,1:T(8,128)S(1)} %get-tuple-element.86, f32[384,512]{0,1:T(8,128)S(1)} %fusion.12, f32[2,512,384]{2,1,0:T(8,128)S(1)} %copy-done.3), kind=kOutput, calls=%fused_computation.22 | convolution fusion | flops 1510195200 | bytes 3080192 | tf_op jit(solution)/shard_map/dot_general | solution.py:29
  191.9 0.9 fusion.27
  192.7 0.9 copy-done.4
  193.6 1.6 fusion.9
  (28 shorter events, 3.5 us)
Async XLA Ops:
  7.2 49.9 %all-gather.3.cloned.1.call-start = ((), (), s32[]{:S(2)}) async-start(), calls=%async_computation | async-start | bytes 1769472 | tf_op jit(solution)/shard_map/all_gather | solution.py:37
  7.9 109.8 %all-gather.5.cloned.1.call-start = ((), (), s32[]{:S(2)}) async-start(), calls=%async_computation.1 | async-start | bytes 3538944 | tf_op jit(solution)/shard_map/all_gather | solution.py:38
  8.6 169.1 %all-reduce.2.cloned.1.call-start = ((), (), s32[]{:S(2)}) async-start(), calls=%async_computation.2 | async-start | bytes 4194304 | tf_op jit(solution)/shard_map/psum | solution.py:25
  10.4 112.5 %collective-permute-start = (f32[256,128]{0,1:T(8,128)}, f32[256,128]{0,1:T(8,128)S(1)}, u32[]{:S(2)}, u32[]{:S(2)}) collective-permute-start(f32[256,128]{0,1:T(8,128)} %copy.13), channel_id=1, source_target_pairs={{0,24},{8,0},{16,8},{24,16},{1,25},{9,1},{17,9},{25,17},{2,26},{10... | collective-permute-start | bytes 393224 | tf_op jit(solution)/shard_map/ppermute | solution.py:17
  12.8 7.7 %collective-permute-start.1 = (f32[256,128]{0,1:T(8,128)}, f32[256,128]{0,1:T(8,128)S(1)}, u32[]{:S(2)}, u32[]{:S(2)}) collective-permute-start(f32[256,128]{0,1:T(8,128)} %copy.13), channel_id=1, source_target_pairs={{0,8},{8,16},{16,24},{24,0},{1,9},{9,17},{17,25},{25,1},{2,10},{10... | collective-permute-start | bytes 393224 | tf_op jit(solution)/shard_map/ppermute | solution.py:15
  20.5 103.6 %collective-permute-start.2 = (f32[256,128]{0,1:T(8,128)S(1)}, f32[256,128]{0,1:T(8,128)}, u32[]{:S(2)}, u32[]{:S(2)}) collective-permute-start(f32[256,128]{0,1:T(8,128)S(1)} %collective-permute-done.1), channel_id=1, source_target_pairs={{0,8},{8,16},{16,24},{24,0},{1,9},{9,17},{17,25},{25,1},{2,10},{10... | collective-permute-start | bytes 393224 | tf_op jit(solution)/shard_map/ppermute | solution.py:15
  118.1 1.3 copy-start.2
  119.5 2.6 %copy-start = (f32[2,1024,384]{2,1,0:T(8,128)S(1)}, f32[2,1024,384]{2,1,0:T(8,128)}, u32[]{:S(2)}) copy-start(f32[2,1024,384]{2,1,0:T(8,128)} %all-gather.5.cloned.1.call-done) | copy-start | bytes 9437188
  121.0 1.2 copy-start.6
  177.8 5.2 %copy-start.3 = (f32[2,512,384]{2,1,0:T(8,128)S(1)}, f32[2,512,384]{2,1,0:T(8,128)}, u32[]{:S(2)}) copy-start(f32[2,512,384]{2,1,0:T(8,128)} %broadcast_multiply_fusion) | copy-start | bytes 4718596
  183.0 2.5 %copy-start.1 = (f32[1024,512]{1,0:T(8,128)S(1)}, f32[1024,512]{1,0:T(8,128)}, u32[]{:S(2)}) copy-start(f32[1024,512]{1,0:T(8,128)} %all-reduce.2.cloned.1.call-done) | copy-start | bytes 6291460
  189.3 2.5 %copy-start.5 = (f32[1024,128]{1,0:T(8,128)S(1)}, f32[1024,128]{1,0:T(8,128)}, u32[]{:S(2)}) copy-start(f32[1024,128]{1,0:T(8,128)} %param.13) | copy-start | bytes 1572868
  191.9 1.8 copy-start.4
Sparse Core Ops, SparseCore 0:
  10.2 46.8 all-gather.2
  59.3 58.3 all-gather.4
  121.2 56.5 all-reduce.1
